TPU v7x, 128 devices: a whole 4x4x4 slice. The times are simulated.
128 devices in a mesh: row: 16 (over z, y_lo, core), col: 8 (over x, y_hi).
Axes of the slice: x: 4, y: 4 (y_hi: 2, y_lo: 2; y = y_hi * 2 + y_lo), z: 4, core: 2. Of those that a mesh axis runs over, the one named last changes fastest.
Arguments:
- hidden_acts: bfloat16 [16384, 29568], P('col', 'row'), may hold values from -6 to 6
- out_grads: bfloat16 [16384, 8192], P('col', 'row'), may hold values from -6 to 6
- proj_in: bfloat16 [29568, 64], P('row'), may hold values from -0.03125 to 0.03125
- proj_out: bfloat16 [8192, 64], P('row'), may hold values from -0.0625 to 0.0625
- white_in: float32 [64, 64], replicated, may hold values from -0.75 to 0.75
- white_out: float32 [64, 64], replicated, may hold values from -0.75 to 0.75
- ep_lengths: int32 [8, 64], P('col'), may hold values from 1 to 64, 2048 in all within a row
- flag_ids: int32 [64], replicated, may hold values from 0 to 511
- train_sketch: bfloat16 [131072, 4096], P('row', 'col'), may hold values from -0.01171875 to 0.01171875
Outputs:
- scores: float32 [64, 131072], P('col', 'row')
Inputs may be any that keep to these rules, and one draw needn't show every extreme that they name: `ep_lengths`: each row holds 64 lengths summing to 2048, the largest exactly 64. `flag_ids`: indices may repeat.
All inputs are finite; a program needn't handle non-finite values.
Results may differ from a plain program's by a relative error of at most 0.0029.
Values may be sent and summed in bfloat16 or wider, within the bound.
A program may use at most 128 MiB of HBM per device.

v0:
```python
import jax
import jax.numpy as jnp
from jax import lax
from jax.sharding import PartitionSpec as P


def episode_sketch(projected, positions, lengths_row, width):
    stops_at = jnp.cumsum(lengths_row)
    starts = stops_at - lengths_row
    member = (
        (positions[None, :] >= starts[:, None]) & (positions[None, :] < stops_at[:, None])
    ).astype(jnp.float32)
    out_part = projected[:, :width]
    in_part = projected[:, width:]
    masked = member[:, :, None] * out_part[None, :, :]
    sketch = jnp.einsum("eto,ti->eoi", masked, in_part, precision=lax.Precision.HIGHEST)
    return sketch.reshape(lengths_row.shape[0], width * width)


def on_device(
    hidden_acts,
    out_grads,
    proj_in,
    proj_out,
    white_in,
    white_out,
    ep_lengths,
    flag_ids,
    train_sketch,
):
    width = proj_in.shape[1]
    tok_rows = hidden_acts.shape[0]
    partial_proj = jnp.concatenate(
        [
            jnp.dot(out_grads, proj_out, preferred_element_type=jnp.float32),
            jnp.dot(hidden_acts, proj_in, preferred_element_type=jnp.float32),
        ],
        axis=1,
    )
    lengths_row = ep_lengths[0]
    full_proj = lax.psum(partial_proj, "row")
    positions = jnp.arange(tok_rows, dtype=jnp.int32)
    sketch = episode_sketch(full_proj, positions, lengths_row, width)
    episodes_here = sketch.shape[0]
    sketch = sketch.reshape(episodes_here, width, width)
    left_side = jnp.einsum("ab,ebc->eac", white_out, sketch, precision=lax.Precision.HIGHEST)
    whitened = jnp.einsum("eac,dc->ead", left_side, white_in, precision=lax.Precision.HIGHEST)
    query_bank = whitened.reshape(episodes_here, width * width).astype(jnp.bfloat16)
    entry_cols = lax.all_to_all(query_bank, "col", split_axis=1, concat_axis=0, tiled=True)
    queries = jnp.take(entry_cols, flag_ids, axis=0)
    return lax.psum_scatter(
        jnp.einsum("fk,tk->ft", queries, train_sketch, preferred_element_type=jnp.float32),
        "col",
        scatter_dimension=0,
        tiled=True,
    )


def solution(mesh):
    in_specs = (
        P("col", "row"),
        P("col", "row"),
        P("row", None),
        P("row", None),
        P(),
        P(),
        P("col", None),
        P(),
        P("row", "col"),
    )
    out_specs = P("col", "row")
    return jax.shard_map(
        on_device, mesh=mesh, in_specs=in_specs, out_specs=out_specs, check_vma=False
    )
```

profile of v0, /device:TPU:1, one launch (start us, length us, event | category | flops | bytes accessed | tf_op | source)
XLA Modules:
  0.0 300.1 jit_solution(7879107046444099900)
XLA Ops:
  6.5 0.0 copy-start
  6.5 0.0 copy-start.1
  6.5 0.0 all-reduce.2.cloned.1.call-start
  6.5 1.6 copy-done
  8.1 1.6 fusion.19
  9.7 0.0 copy-done.1
  9.7 4.6 %fusion.20 = f32[2048,64]{0,1:T(8,128)S(1)} fusion(bf16[2048,1848]{0,1:T(8,128)(2,1)} %param.9, bf16[1848,64]{0,1:T(8,128)(2,1)S(1)} %copy-done.1), kind=kOutput, calls=%fused_computation.27 | convolution fusion | flops 484442112 | bytes 8330240 | tf_op jit(solution)/shard_map/dot_general | solution.py:36
  14.3 0.0 copy-start.4
  14.4 1.1 pad_maximum_fusion
  15.5 0.0 all-reduce.2.cloned.1.call-update
  15.5 0.0 copy-done.4
  15.5 0.1 copy.16
  15.6 0.1 reduce-window.7
  15.7 0.1 reduce
  15.8 0.2 fusion.10
  16.0 122.5 %all-reduce.2.cloned.1.call-done = f32[2048,128]{0,1:T(8,128)} async-done(((f32[2048,128]{0,1:T(8,128)}), f32[2048,128]{0,1:T(8,128)}) %all-reduce.2.cloned.1.call-update) | async-done | bytes 1048592 | tf_op jit(solution)/shard_map/psum | solution.py:41
  138.6 1.1 slice.10
  139.6 0.0 copy-start.2
  139.6 49.9 %fusion = f32[64,64,64]{1,2,0:T(8,128)S(1)} fusion(f32[2048,64]{0,1:T(8,128)S(1)} %slice.10, f32[64,2048]{1,0:T(8,128)S(1)} %fusion.10, f32[2048,128]{0,1:T(8,128)} %all-reduce.2.cloned.1.call-done), kind=kOutput, calls=%fused_computation.1 | convolution fusion | flops 6450839552 | bytes 2621440 | tf_op jit(solution)/shard_map/eto,ti->eoi/dot_general | solution.py:16
  189.6 0.0 copy-done.2
  189.6 0.0 copy-start.3
  189.6 1.9 fusion.15
  191.5 0.0 copy-done.3
  191.5 3.5 %fusion.6 = bf16[64,64,64]{2,1,0:T(8,128)(2,1)S(1)} fusion(f32[64,64,64]{2,1,0:T(8,128)S(1)} %fusion.15, f32[64,64]{1,0:T(8,128)S(1)} %copy-done.3), kind=kOutput, calls=%fused_computation.7 | convolution fusion | flops 201588736 | bytes 1589248 | tf_op jit(solution)/shard_map/eac,dc->ead/dot_general | solution.py:47
  195.0 0.0 copy-start.5
  195.0 1.4 convert_element_type.16
  196.4 2.0 copy.19
  198.4 6.1 %all-to-all-start = ((bf16[64,8,512]{2,0,1:T(8,128)(2,1)}), bf16[64,8,512]{2,0,1:T(8,128)(2,1)S(1)}, u32[]{:S(2)}, u32[]{:S(2)}) async-start(bf16[64,8,512]{2,0,1:T(8,128)(2,1)} %copy.19), calls=%async_computation | async-start | bytes 1048576 | tf_op jit(solution)/shard_map/all_to_all | solution.py:49
  204.5 0.0 reduce-scatter.2.cloned.1.call-start
  204.6 0.0 copy-done.5
  204.6 8.9 %all-to-all-done = bf16[64,8,512]{2,0,1:T(8,128)(2,1)S(1)} async-done(((bf16[64,8,512]{2,0,1:T(8,128)(2,1)}), bf16[64,8,512]{2,0,1:T(8,128)(2,1)S(1)}, u32[]{:S(2)}, u32[]{:S(2)}) %all-to-all-start) | async-done | bytes 524320 | tf_op jit(solution)/shard_map/all_to_all | solution.py:49
  213.6 0.7 gather_fusion
  214.3 7.4 %fusion.11 = f32[64,8192]{1,0:T(8,128)} fusion(bf16[8192,512]{1,0:T(8,128)(2,1)} %param.17, bf16[64,512]{1,0:T(8,128)(2,1)S(1)} %gather_fusion, pred[64]{0:T(512)(128)(4,1)S(1)} %compare_and_fusion), kind=kOutput, calls=%fused_computation.14 | convolution fusion | flops 536903680 | bytes 10551360 | tf_op jit(solution)/shard_map/fk,tk->ft/dot_general | solution.py:52
  221.6 0.0 reduce-scatter.2.cloned.1.call-update
  221.7 71.6 %reduce-scatter.2.cloned.1.call-done = f32[8,8192]{1,0:T(8,128)} async-done(((f32[64,8192]{1,0:T(8,128)}), f32[8,8192]{1,0:T(8,128)}) %reduce-scatter.2.cloned.1.call-update) | async-done | bytes 262160 | tf_op jit(solution)/shard_map/reduce_scatter | solution.py:51
  (4 shorter events, 0.0 us)
Async XLA Ops:
  6.5 1.6 copy-start
  6.5 3.2 %copy-start.1 = (bf16[1848,64]{0,1:T(8,128)(2,1)S(1)}, bf16[1848,64]{0,1:T(8,128)(2,1)}, u32[]{:S(2)}) copy-start(bf16[1848,64]{0,1:T(8,128)(2,1)} %param.11) | copy-start | bytes 709636
  6.5 132.0 %all-reduce.2.cloned.1.call-start = ((), (), s32[]{:S(2)}) async-start(), calls=%async_computation.2 | async-start | bytes 2097152 | tf_op jit(solution)/shard_map/psum | solution.py:41
  14.3 1.1 copy-start.4
  139.6 50.0 %copy-start.2 = (f32[64,64]{1,0:T(8,128)S(1)}, f32[64,64]{1,0:T(8,128)}, u32[]{:S(2)}) copy-start(f32[64,64]{1,0:T(8,128)} %param.14) | copy-start | bytes 49156
  189.6 1.9 copy-start.3
  195.0 9.6 %copy-start.5 = (s32[64]{0:T(128)S(1)}, s32[64]{0:T(128)}, u32[]{:S(2)}) copy-start(s32[64]{0:T(128)} %param.16) | copy-start | bytes 772
  198.4 15.2 %all-to-all-start = ((bf16[64,8,512]{2,0,1:T(8,128)(2,1)}), bf16[64,8,512]{2,0,1:T(8,128)(2,1)S(1)}, u32[]{:S(2)}, u32[]{:S(2)}) async-start(bf16[64,8,512]{2,0,1:T(8,128)(2,1)} %copy.19), calls=%async_computation | async-start | bytes 1048576 | tf_op jit(solution)/shard_map/all_to_all | solution.py:49
  204.5 88.7 %reduce-scatter.2.cloned.1.call-start = ((), (), s32[]{:S(2)}) async-start(), calls=%async_computation.3 | async-start | bytes 2359296 | tf_op jit(solution)/shard_map/reduce_scatter | solution.py:51
Sparse Core Ops, SparseCore 0:
  15.6 122.9 all-reduce.1
  221.8 71.3 reduce-scatter.1
where the time goes:
time: 301 us; the launch traced here: 300 us
  waiting for transfers between devices  203 us (67%)
  matrix products  68.9 us (23%)
  between operations  13.6 us (5%)
  local copies, waits for them, and re-layouts  6.88 us (2%)
  starting transfers between devices  6.17 us (2%)
    psum x1, waiting for transfers between devices, on_device(): full_proj = lax.psum(partial_proj, 'row')  123 us
    reduce_scatter x1, waiting for transfers between devices, on_device(): lax.psum_scatter(jnp.einsum('fk,tk->ft', queries, train_sketch, preferred...  71.6 us
    dot_general x1, matrix products, episode_sketch(): jnp.einsum('eto,ti->eoi', masked, in_part, precision=lax.Precision.HIGHEST)  49.9 us
    all_to_all x1, waiting for transfers between devices, on_device(): lax.all_to_all(query_bank, 'col', split_axis=1, concat_axis=0, tiled=True)  8.94 us
    dot_general x1, matrix products, on_device(): jnp.einsum('fk,tk->ft', queries, train_sketch, preferred_element_type=jnp...  7.37 us
    all_to_all x1, starting transfers between devices, on_device(): lax.all_to_all(query_bank, 'col', split_axis=1, concat_axis=0, tiled=True)  6.13 us
  transfers between devices with their start and end apart: 3, of which 3 were waited for; matrix products, arithmetic and copies ran while one was open for 0% of the time, Pallas kernels for 0%

commit v1 on v0

v1 whole, which is shorter than its diff:
```python
import jax
import jax.numpy as jnp
from jax import lax
from jax.experimental import pallas as pl
from jax.experimental.pallas import tpu as pltpu
from jax.sharding import PartitionSpec as P

MESH = pl.DeviceIdType.MESH
F32 = jnp.float32
BF16 = jnp.bfloat16
NT = (((1,), (1,)), ((), ()))
NN = (((1,), (0,)), ((), ()))
CHUNKS = 8


def hdot(a, b, dims):
    return lax.dot_general(a, b, dims, precision=lax.Precision.HIGHEST, preferred_element_type=F32)


def windows(lens, flags, g_ref, h_ref, out_ref, starts):
    col = lax.axis_index("col")

    def count(k, total):
        starts[k] = total
        return total + lens[0, k]

    lax.fori_loop(0, 64, count, jnp.int32(0))
    lane = lax.broadcasted_iota(jnp.int32, (64, 128), 1)

    def place(f):
        k = flags[f] - 64 * col
        inside = (k >= 0) & (k < 64)
        k = jnp.where(inside, k, 0)
        return starts[k], jnp.where(inside, lens[0, k], 0)

    def window(ref, start, at):
        first = start // 128
        off = start - first * 128
        a = ref[:, pl.ds(pl.multiple_of(first * 128, 128), 128)]
        second = jnp.minimum(first + 1, 15)
        b = ref[:, pl.ds(pl.multiple_of(second * 128, 128), 128)]
        shift = (at + 128 - off) % 128
        a = pltpu.roll(a, shift, 1)
        b = pltpu.roll(b, shift, 1)
        return jnp.where(lane - at + off < 128, a, b)

    def pair(j, _):
        sa, la = place(2 * j)
        sb, lb = place(2 * j + 1)
        keep = lane < jnp.where(lane < 64, la, lb + 64)
        for at, ref in ((0, g_ref), (64, h_ref)):
            both = jnp.where(lane < 64, window(ref, sa, 0), window(ref, sb, 64))
            out_ref[j, pl.ds(at, 64), :] = jnp.where(keep, both, 0.0)
        return 0

    lax.fori_loop(0, 32, pair, 0)


def kernel(
    w_ref, wi_ref, wo_ref, train_hbm, out_ref,
    train, acc, got, peers, rows, mix, tiles_out, tiles_in, mine, every, query,
    part, send, recv,
    t_sem, w_sem, s0, r0, s1, r1, s2, r2, s3, r3, s4, r4,
):
    row = lax.axis_index("row")
    col = lax.axis_index("col")
    chip = row // 2
    core = row % 2
    n_train = train.shape[0]
    half = n_train // 2
    width = half // CHUNKS
    block = n_train // CHUNKS

    def fetch(k):
        at = pl.ds(k * block, block)
        return pltpu.make_async_copy(train_hbm.at[at, :], train.at[at, :], t_sem.at[k])

    def keep(q):
        return pltpu.make_async_copy(w_ref.at[pl.ds(4 * q + 2 * core, 2)], acc.at[q], w_sem.at[q])

    barrier = pltpu.get_barrier_semaphore()
    for d in range(1, 16):
        pl.semaphore_signal(barrier, inc=1, device_id={"row": (row + d) % 16}, device_id_type=MESH)
    for d in range(1, 8):
        pl.semaphore_signal(barrier, inc=1, device_id={"col": (col + d) % 8}, device_id_type=MESH)

    def copy0(q):
        return pltpu.make_async_remote_copy(
            src_ref=w_ref.at[pl.ds(4 * q + 2 * (1 - core), 2)], dst_ref=got.at[q], send_sem=s0.at[q], recv_sem=r0.at[q],
            device_id={"row": row + 1 - 2 * core}, device_id_type=MESH)

    def copy1(d):
        q = (chip + d) % 8
        return pltpu.make_async_remote_copy(
            src_ref=acc.at[q], dst_ref=peers.at[d - 1], send_sem=s1.at[d - 1], recv_sem=r1.at[d - 1],
            device_id={"row": 2 * q + core}, device_id_type=MESH)

    def copy2(d):
        c = (col + d) % 8
        return pltpu.make_async_remote_copy(
            src_ref=tiles_out.at[c], dst_ref=tiles_in.at[d - 1], send_sem=s2.at[d - 1], recv_sem=r2.at[d - 1],
            device_id={"col": c}, device_id_type=MESH)

    def copy3(d):
        return pltpu.make_async_remote_copy(
            src_ref=mine, dst_ref=every.at[row], send_sem=s3.at[d - 1], recv_sem=r3.at[d - 1],
            device_id={"row": (row + d) % 16}, device_id_type=MESH)

    def copy4(d, j):
        c = (col + d) % 8
        at = pl.ds(pl.multiple_of(j * width, width), width)
        return pltpu.make_async_remote_copy(
            src_ref=send.at[c, :, at], dst_ref=recv.at[d - 1, :, at],
            send_sem=s4.at[d - 1, j], recv_sem=r4.at[d - 1, j],
            device_id={"col": c}, device_id_type=MESH)

    pl.semaphore_wait(barrier, 22)

    for d in (4, 3, 5, 2, 6, 1, 7, 0):
        copy0((chip + d) % 8).start()
    for q in range(8):
        keep(q).start()
    for k in range(CHUNKS):
        fetch(k).start()
    for q in range(8):
        keep(q).wait()
    for d in (4, 3, 5, 2, 6, 1, 7, 0):
        q = (chip + d) % 8
        copy0(q).wait_recv()
        acc[q] = acc[q] + got[q]
        if d:
            copy1(d).start()
    for d in (1, 7, 2, 6, 3, 5, 4):
        copy1(d).wait_recv()

    for p in range(2):
        total = acc[chip, p]
        for d in range(7):
            total = total + peers[d, p]
        mix[...] = hdot(wo_ref[...], total[:64], NN)
        hw = hdot(wi_ref[...], total[64:], NN)
        hw = jnp.concatenate([hw, hw], axis=0)
        even = mix[pl.ds(0, 32, 2), :]
        odd = mix[pl.ds(1, 32, 2), :]
        low = lax.broadcasted_iota(jnp.int32, (32, 128), 1) < 64
        for u in range(2):
            if u == 0:
                ev, od = jnp.where(low, even, 0.0), jnp.where(low, odd, 0.0)
            else:
                ev, od = jnp.where(low, 0.0, even), jnp.where(low, 0.0, odd)
            qe = hdot(ev, hw, NT)
            qo = hdot(od, hw, NT)
            rows[pl.ds(2 * p + u, 32, 4), :] = jnp.where(low, qe, qo)
    tiles_out[...] = rows[...].astype(BF16).reshape(8, 16, 128)
    for d in range(1, 8):
        copy2(d).start()
    tile = tiles_out[col].astype(F32)
    for d in range(1, 8):
        copy2(d).wait_recv()
        tile = tile + tiles_in[d - 1].astype(F32)
    tile = tile.astype(BF16)
    mine[...] = tile
    for d in range(1, 16):
        copy3(d).start()
    every[row] = tile
    for d in range(1, 16):
        copy3(d).wait_recv()

    flat = every[...].reshape(256, 128)
    to = lax.broadcasted_iota(jnp.int32, (64, 256), 0)
    frm = lax.broadcasted_iota(jnp.int32, (64, 256), 1)
    for a in range(4):
        perm = jnp.where(frm == (to // 4) * 16 + 4 * a + to % 4, 1.0, 0.0).astype(BF16)
        query[:, 128 * a:128 * (a + 1)] = lax.dot_general(perm, flat, NN, preferred_element_type=F32).astype(BF16)

    for k in range(CHUNKS):
        fetch(k).wait()

    def score(j, _):
        lo = pl.multiple_of(j * width, width)
        hi = pl.multiple_of(half + j * width, width)
        own = pl.ds(pl.multiple_of(col * 8, 8), 8)
        a = lax.dot_general(query[...], train[pl.ds(lo, width), :], NT, preferred_element_type=F32)
        b = lax.dot_general(query[...], train[pl.ds(hi, width), :], NT, preferred_element_type=F32)
        for c in range(8):
            both = jnp.concatenate([a[8 * c:8 * c + 8], b[8 * c:8 * c + 8]], axis=0)
            send[c, :, pl.ds(lo, width)] = both.astype(BF16)
        for d in (4, 3, 5, 2, 6, 1, 7):
            copy4(d, j).start()
        part[...] = a
        out_ref[:, pl.ds(lo, width)] = part[own, :]
        part[...] = b
        out_ref[:, pl.ds(hi, width)] = part[own, :]
        return 0

    lax.fori_loop(0, CHUNKS, score, 0)

    def collect(j, _):
        lo = pl.ds(pl.multiple_of(j * width, width), width)
        hi = pl.ds(pl.multiple_of(half + j * width, width), width)
        both = jnp.concatenate([out_ref[:, lo], out_ref[:, hi]], axis=0)
        for d in range(1, 8):
            copy4(d, j).wait_recv()
            both = both + recv[d - 1, :, lo].astype(F32)
        out_ref[:, lo] = both[:8]
        out_ref[:, hi] = both[8:]
        return 0

    lax.fori_loop(0, CHUNKS, collect, 0)

    def sent0(q, _):
        copy0(q).wait_send()
        return 0

    lax.fori_loop(0, 8, sent0, 0)
    for d in range(1, 8):
        copy1(d).wait_send()
        copy2(d).wait_send()
    for d in range(1, 16):
        copy3(d).wait_send()

    def sent4(j, _):
        for d in range(1, 8):
            copy4(d, j).wait_send()
        return 0

    lax.fori_loop(0, CHUNKS, sent4, 0)


def on_device(hidden_acts, out_grads, proj_in, proj_out, white_in, white_out, ep_lengths, flag_ids, train_sketch):
    across = (((0,), (1,)), ((), ()))
    g_t = lax.dot_general(proj_out, out_grads, across, preferred_element_type=F32)
    h_t = lax.dot_general(proj_in, hidden_acts, across, preferred_element_type=F32)
    n_train, depth = train_sketch.shape
    vmem = pl.BlockSpec(memory_space=pltpu.VMEM)
    smem = pl.BlockSpec(memory_space=pltpu.SMEM)
    dma = pltpu.SemaphoreType.DMA
    w = pl.pallas_call(
        windows,
        out_shape=jax.ShapeDtypeStruct((32, 128, 128), F32),
        in_specs=[smem, smem, vmem, vmem],
        out_specs=vmem,
        scratch_shapes=[pltpu.SMEM((64,), jnp.int32)],
        name="windows",
    )(ep_lengths, flag_ids, g_t, h_t)
    hbm = pl.BlockSpec(memory_space=pl.ANY)
    return pl.pallas_call(
        kernel,
        out_shape=jax.ShapeDtypeStruct((8, n_train), F32),
        in_specs=[hbm, vmem, vmem, hbm],
        out_specs=vmem,
        scratch_shapes=[
            pltpu.VMEM((n_train, depth), BF16),
            pltpu.VMEM((8, 2, 128, 128), F32),
            pltpu.VMEM((8, 2, 128, 128), F32),
            pltpu.VMEM((7, 2, 128, 128), F32),
            pltpu.VMEM((128, 128), F32),
            pltpu.VMEM((64, 128), F32),
            pltpu.VMEM((8, 16, 128), BF16),
            pltpu.VMEM((7, 16, 128), BF16),
            pltpu.VMEM((16, 128), BF16),
            pltpu.VMEM((16, 16, 128), BF16),
            pltpu.VMEM((64, depth), BF16),
            pltpu.VMEM((64, n_train // 2 // CHUNKS), F32),
            pltpu.VMEM((8, 16, n_train // 2), BF16),
            pltpu.VMEM((7, 16, n_train // 2), BF16),
            dma((CHUNKS,)), dma((8,)),
            dma((8,)), dma((8,)),
            dma((7,)), dma((7,)),
            dma((7,)), dma((7,)),
            dma((15,)), dma((15,)),
            dma((7, CHUNKS)), dma((7, CHUNKS)),
        ],
        compiler_params=pltpu.CompilerParams(collective_id=0, has_side_effects=True),
        name="attribute",
    )(w, white_in, white_out, train_sketch)


def solution(mesh):
    in_specs = (
        P("col", "row"), P("col", "row"), P("row", None), P("row", None), P(), P(),
        P("col", None), P(), P("row", "col"),
    )
    return jax.shard_map(on_device, mesh=mesh, in_specs=in_specs, out_specs=P("col", "row"), check_vma=False)
```

time: 301 us -> 72 us (0.24)
  waiting for transfers between devices: 203 us -> 0 us
  Pallas kernels: 0 us -> 62.7 us
  matrix products: 68.9 us -> 7.39 us
  between operations: 13.6 us -> 0.01 us
  starting transfers between devices: 6.17 us -> 0 us
  local copies, waits for them, and re-layouts: 6.88 us -> 1.68 us
    psum x1 -> x0, waiting for transfers between devices: 123 us -> none  [on_device(): full_proj = lax.psum(partial_proj, 'row')]
    reduce_scatter x1 -> x0, waiting for transfers between devices: 71.6 us -> none  [on_device(): lax.psum_scatter(jnp.einsum('fk,tk->ft', queries, train_sketch, preferred...]
    pallas_call x0 -> x2, Pallas kernels: none -> 62.7 us  [the longest x1 54.9 us: on_device(): pl.pallas_call(kernel, out_shape=jax.ShapeDtypeStruct((8, n_train), F32),...]
    dot_general x6 -> x2, matrix products: 68.9 us -> 7.39 us  [the longest x1 5.84 us: on_device(): lax.dot_general(proj_in, hidden_acts, across, preferred_element_type=F32)]
    all_to_all x1 -> x0, waiting for transfers between devices: 8.94 us -> none  [on_device(): lax.all_to_all(query_bank, 'col', split_axis=1, concat_axis=0, tiled=True)]
    all_to_all x1 -> x0, starting transfers between devices: 6.13 us -> none  [on_device(): lax.all_to_all(query_bank, 'col', split_axis=1, concat_axis=0, tiled=True)]
    convert_element_type x2 -> x0, local copies, waits for them, and re-layouts: 3.4 us -> none  [on_device(): whitened.reshape(episodes_here, width * width).astype(jnp.bfloat16)]
  transfers between devices with their start and end apart: 3 -> 0, of which waited for: 3 -> 0; matrix products, arithmetic and copies ran while one was open for 0% -> 0% of each run, Pallas kernels for 0% -> 0%
where the time goes in v1:
time: 72 us; the launch traced here: 71.8 us
  Pallas kernels  62.7 us (87%)
  matrix products  7.39 us (10%)
  local copies, waits for them, and re-layouts  1.68 us (2%)
    pallas_call x1, Pallas kernels, on_device(): pl.pallas_call(kernel, out_shape=jax.ShapeDtypeStruct((8, n_train), F32),...  54.9 us
    pallas_call x1, Pallas kernels, on_device(): pl.pallas_call(windows, out_shape=jax.ShapeDtypeStruct((32, 128, 128), F3...  7.82 us
    dot_general x1, matrix products, on_device(): lax.dot_general(proj_in, hidden_acts, across, preferred_element_type=F32)  5.84 us
    unnamed x5, local copies, waits for them, and re-layouts  1.68 us
    dot_general x1, matrix products, on_device(): lax.dot_general(proj_out, out_grads, across, preferred_element_type=F32)  1.55 us

profile of v1, /device:TPU:1, one launch (start us, length us, event | category | flops | bytes accessed | tf_op | source)
XLA Modules:
  0.0 71.8 jit_solution(8198870429375839335)
XLA Ops:
  0.0 0.0 copy-start
  0.0 0.0 copy-start.1
  0.0 5.8 %fusion.1.h_ref = f32[64,2048]{1,0:T(8,128)} fusion(bf16[1848,64]{0,1:T(8,128)(2,1)} %param.11, bf16[2048,1848]{0,1:T(8,128)(2,1)} %param.9), kind=kOutput, calls=%fused_computation.1 | convolution fusion | flops 484442112 | bytes 8330240 | tf_op jit(solution)/shard_map/dot_general | solution.py:233
  5.8 0.0 copy-done
  5.8 0.0 copy-done.1
  5.9 1.5 %fusion.g_ref = f32[64,2048]{1,0:T(8,128)} fusion(bf16[512,64]{0,1:T(8,128)(2,1)S(1)} %copy-done.1, bf16[2048,512]{1,0:T(8,128)(2,1)S(1)} %copy-done), kind=kOutput, calls=%fused_computation | convolution fusion | flops 134217728 | bytes 2686976 | tf_op jit(solution)/shard_map/dot_general | solution.py:232
  7.4 7.8 %windows.1.w_ref = f32[32,128,128]{2,1,0:T(8,128)} custom-call(s32[1,64]{1,0:T(1,128)} %lens.1, s32[64]{0:T(128)} %flags.1, f32[64,2048]{1,0:T(8,128)} %fusion.g_ref, f32[64,2048]{1,0:T(8,128)} %fusion.1.h_ref), custom_call_target="tpu_custom_call" | custom-call | tf_op jit(solution)/shard_map/windows/pallas_call | solution.py:238
  15.2 54.9 %attribute.1 = f32[8,8192]{1,0:T(8,128)} custom-call(f32[32,128,128]{2,1,0:T(8,128)} %windows.1.w_ref, f32[64,64]{1,0:T(8,128)} %wi_ref.1, f32[64,64]{1,0:T(8,128)} %wo_ref.1, bf16[8192,512]{1,0:T(8,128)(2,1)} %train_hbm.1), custom_call_target="tpu_custom_call" | custom-call | tf_op jit(solution)/shard_map/attribute/pallas_call | solution.py:247
  70.1 1.7 %copy.11 = f32[8,8192]{1,0:T(8,128)} copy(f32[8,8192]{1,0:T(8,128)} %attribute.1) | data formatting | bytes 524288
Async XLA Ops:
  0.0 5.8 %copy-start = (bf16[2048,512]{1,0:T(8,128)(2,1)S(1)}, bf16[2048,512]{1,0:T(8,128)(2,1)}, u32[]{:S(2)}) copy-start(bf16[2048,512]{1,0:T(8,128)(2,1)} %param.10) | copy-start | bytes 6291460
  0.0 5.8 %copy-start.1 = (bf16[512,64]{0,1:T(8,128)(2,1)S(1)}, bf16[512,64]{0,1:T(8,128)(2,1)}, u32[]{:S(2)}) copy-start(bf16[512,64]{0,1:T(8,128)(2,1)} %param.12) | copy-start | bytes 196612

commit v2 on v1

--- a/solution.py
+++ b/solution.py
@@ -17,48 +17,55 @@
     return lax.dot_general(a, b, dims, precision=lax.Precision.HIGHEST, preferred_element_type=F32)
 
 
-def windows(lens, flags, g_ref, h_ref, out_ref, starts):
+def windows(lens, flags, pin_ref, pout_ref, acts_hbm, grads_hbm, out_ref, starts, acts, grads, gh, a_sem, g_sem):
     col = lax.axis_index("col")
+    few = acts.shape[2]
+    tokens = CHUNKS * few
+
+    def bring(k):
+        at = pl.ds(k * few, few)
+        return (pltpu.make_async_copy(acts_hbm.at[:, at], acts.at[k], a_sem.at[k]),
+                pltpu.make_async_copy(grads_hbm.at[at, :], grads.at[at, :], g_sem.at[k]))
+
+    for k in range(CHUNKS):
+        for copy in bring(k):
+            copy.start()
 
     def count(k, total):
         starts[k] = total
         return total + lens[0, k]
 
     lax.fori_loop(0, 64, count, jnp.int32(0))
-    lane = lax.broadcasted_iota(jnp.int32, (64, 128), 1)
-
-    def place(f):
+    gh[pl.ds(tokens, 64), :] = jnp.zeros((64, 128), F32)
+
+    for k in range(CHUNKS):
+        for copy in bring(k):
+            copy.wait()
+        at = pl.ds(k * few, few)
+        g = lax.dot_general(pout_ref[...], grads[at, :], NT, preferred_element_type=F32)
+        h = lax.dot_general(pin_ref[...], acts[k], NN, preferred_element_type=F32)
+        gh[at, :] = jnp.concatenate([g, h], axis=0).T
+
+    token = lax.broadcasted_iota(jnp.int32, (64, 128), 0)
+
+    def window(f):
         k = flags[f] - 64 * col
         inside = (k >= 0) & (k < 64)
         k = jnp.where(inside, k, 0)
-        return starts[k], jnp.where(inside, lens[0, k], 0)
-
-    def window(ref, start, at):
-        first = start // 128
-        off = start - first * 128
-        a = ref[:, pl.ds(pl.multiple_of(first * 128, 128), 128)]
-        second = jnp.minimum(first + 1, 15)
-        b = ref[:, pl.ds(pl.multiple_of(second * 128, 128), 128)]
-        shift = (at + 128 - off) % 128
-        a = pltpu.roll(a, shift, 1)
-        b = pltpu.roll(b, shift, 1)
-        return jnp.where(lane - at + off < 128, a, b)
+        n = jnp.where(inside, lens[0, k], 0)
+        return jnp.where(token < n, gh[pl.ds(starts[k], 64), :], 0.0)
 
     def pair(j, _):
-        sa, la = place(2 * j)
-        sb, lb = place(2 * j + 1)
-        keep = lane < jnp.where(lane < 64, la, lb + 64)
-        for at, ref in ((0, g_ref), (64, h_ref)):
-            both = jnp.where(lane < 64, window(ref, sa, 0), window(ref, sb, 64))
-            out_ref[j, pl.ds(at, 64), :] = jnp.where(keep, both, 0.0)
-        return 0
-
-    lax.fori_loop(0, 32, pair, 0)
+        for u in range(2):
+            out_ref[j, pl.ds(64 * u, 64), :] = window(2 * j + u)
+        return 0
+
+    lax.fori_loop(0, 32, pair, 0, unroll=4)
 
 
 def kernel(
     w_ref, wi_ref, wo_ref, train_hbm, out_ref,
-    train, acc, got, peers, rows, mix, tiles_out, tiles_in, mine, every, query,
+    train, acc, got, peers, rows, tiles_out, tiles_in, mine, every, query,
     part, send, recv,
     t_sem, w_sem, s0, r0, s1, r1, s2, r2, s3, r3, s4, r4,
 ):
@@ -133,24 +140,21 @@
     for d in (1, 7, 2, 6, 3, 5, 4):
         copy1(d).wait_recv()
 
+    none = jnp.zeros((64, 64), F32)
+    wi = jnp.concatenate([none, wi_ref[...]], axis=1)
+    wi = jnp.concatenate([wi, wi], axis=0)
+    wo = jnp.concatenate([wo_ref[pl.ds(0, 32, 2), :], wo_ref[pl.ds(1, 32, 2), :]], axis=0)
+    wo = jnp.concatenate([wo, none], axis=1)
+    low = lax.broadcasted_iota(jnp.int32, (64, 128), 1) < 64
     for p in range(2):
         total = acc[chip, p]
         for d in range(7):
             total = total + peers[d, p]
-        mix[...] = hdot(wo_ref[...], total[:64], NN)
-        hw = hdot(wi_ref[...], total[64:], NN)
-        hw = jnp.concatenate([hw, hw], axis=0)
-        even = mix[pl.ds(0, 32, 2), :]
-        odd = mix[pl.ds(1, 32, 2), :]
-        low = lax.broadcasted_iota(jnp.int32, (32, 128), 1) < 64
+        gw = hdot(wo, total, NT)
+        hw = hdot(total, wi, NT)
         for u in range(2):
-            if u == 0:
-                ev, od = jnp.where(low, even, 0.0), jnp.where(low, odd, 0.0)
-            else:
-                ev, od = jnp.where(low, 0.0, even), jnp.where(low, 0.0, odd)
-            qe = hdot(ev, hw, NT)
-            qo = hdot(od, hw, NT)
-            rows[pl.ds(2 * p + u, 32, 4), :] = jnp.where(low, qe, qo)
+            both = hdot(jnp.where(low if u == 0 else ~low, gw, 0.0), hw, NN)
+            rows[pl.ds(2 * p + u, 32, 4), :] = jnp.where(low[:32], both[:32], both[32:])
     tiles_out[...] = rows[...].astype(BF16).reshape(8, 16, 128)
     for d in range(1, 8):
         copy2(d).start()
@@ -228,22 +232,27 @@
 
 
 def on_device(hidden_acts, out_grads, proj_in, proj_out, white_in, white_out, ep_lengths, flag_ids, train_sketch):
-    across = (((0,), (1,)), ((), ()))
-    g_t = lax.dot_general(proj_out, out_grads, across, preferred_element_type=F32)
-    h_t = lax.dot_general(proj_in, hidden_acts, across, preferred_element_type=F32)
+    tokens, width = hidden_acts.shape
+    model = out_grads.shape[1]
     n_train, depth = train_sketch.shape
     vmem = pl.BlockSpec(memory_space=pltpu.VMEM)
     smem = pl.BlockSpec(memory_space=pltpu.SMEM)
     dma = pltpu.SemaphoreType.DMA
+    hbm = pl.BlockSpec(memory_space=pl.ANY)
     w = pl.pallas_call(
         windows,
         out_shape=jax.ShapeDtypeStruct((32, 128, 128), F32),
-        in_specs=[smem, smem, vmem, vmem],
+        in_specs=[smem, smem, vmem, vmem, hbm, hbm],
         out_specs=vmem,
-        scratch_shapes=[pltpu.SMEM((64,), jnp.int32)],
+        scratch_shapes=[
+            pltpu.SMEM((64,), jnp.int32),
+            pltpu.VMEM((CHUNKS, width, tokens // CHUNKS), BF16),
+            pltpu.VMEM((tokens, model), BF16),
+            pltpu.VMEM((tokens + 64, 128), F32),
+            dma((CHUNKS,)), dma((CHUNKS,)),
+        ],
         name="windows",
-    )(ep_lengths, flag_ids, g_t, h_t)
-    hbm = pl.BlockSpec(memory_space=pl.ANY)
+    )(ep_lengths, flag_ids, proj_in.T, proj_out.T, hidden_acts.T, out_grads)
     return pl.pallas_call(
         kernel,
         out_shape=jax.ShapeDtypeStruct((8, n_train), F32),
@@ -255,7 +264,6 @@
             pltpu.VMEM((8, 2, 128, 128), F32),
             pltpu.VMEM((7, 2, 128, 128), F32),
             pltpu.VMEM((128, 128), F32),
-            pltpu.VMEM((64, 128), F32),
             pltpu.VMEM((8, 16, 128), BF16),
             pltpu.VMEM((7, 16, 128), BF16),
             pltpu.VMEM((16, 128), BF16),

time: 72 us -> 65.2 us (0.906)
  matrix products: 7.39 us -> 0 us
    dot_general x2 -> x0, matrix products: 7.39 us -> none  [the longest x1 5.84 us: on_device(): lax.dot_general(proj_in, hidden_acts, across, preferred_element_type=F32)]
    pallas_call x1, Pallas kernels: 7.82 us -> 8.55 us  [on_device(): pl.pallas_call(windows, out_shape=jax.ShapeDtypeStruct((32, 128, 128), F3...]
    unnamed x5 -> x1, local copies, waits for them, and re-layouts: 1.68 us -> 1.67 us
where the time goes in v2:
time: 65.2 us; the launch traced here: 65 us
  Pallas kernels  63.3 us (97%)
  local copies, waits for them, and re-layouts  1.67 us (3%)
    pallas_call x1, Pallas kernels, on_device(): pl.pallas_call(kernel, out_shape=jax.ShapeDtypeStruct((8, n_train), F32),...  54.8 us
    pallas_call x1, Pallas kernels, on_device(): pl.pallas_call(windows, out_shape=jax.ShapeDtypeStruct((32, 128, 128), F3...  8.55 us
    unnamed x1, local copies, waits for them, and re-layouts  1.67 us

profile of v2, /device:TPU:1, one launch (start us, length us, event | category | flops | bytes accessed | tf_op | source)
XLA Modules:
  0.0 65.0 jit_solution(14265145191611635331)
XLA Ops:
  0.0 8.6 %windows.1.w_ref = f32[32,128,128]{2,1,0:T(8,128)} custom-call(s32[1,64]{1,0:T(1,128)} %lens.1, s32[64]{0:T(128)} %flags.1, bf16[64,1848]{1,0:T(8,128)(2,1)} %bitcast.4, bf16[64,512]{1,0:T(8,128)(2,1)} %bitcast.5, bf16[1848,2048]{1,0:T(8,128)(2,1)} %bitcast.3, bf16[2048,512]{1,0:T(8,128)(2,1)} %grads_hbm.1), custom_call_target="tpu_custom_call" | custom-call | tf_op jit(solution)/shard_map/windows/pallas_call | solution.py:242
  8.6 54.8 %attribute.1 = f32[8,8192]{1,0:T(8,128)} custom-call(f32[32,128,128]{2,1,0:T(8,128)} %windows.1.w_ref, f32[64,64]{1,0:T(8,128)} %wi_ref.1, f32[64,64]{1,0:T(8,128)} %wo_ref.1, bf16[8192,512]{1,0:T(8,128)(2,1)} %train_hbm.1), custom_call_target="tpu_custom_call" | custom-call | tf_op jit(solution)/shard_map/attribute/pallas_call | solution.py:256
  63.3 1.7 %copy.11 = f32[8,8192]{1,0:T(8,128)} copy(f32[8,8192]{1,0:T(8,128)} %attribute.1) | data formatting | bytes 524288

commit v3 on v2

--- a/solution.py
+++ b/solution.py
@@ -65,9 +65,9 @@
 
 def kernel(
     w_ref, wi_ref, wo_ref, train_hbm, out_ref,
-    train, acc, got, peers, rows, tiles_out, tiles_in, mine, every, query,
+    train, acc, got, coded, unit, codes, units, rows, tiles_out, tiles_in, mine, every, query,
     part, send, recv,
-    t_sem, w_sem, s0, r0, s1, r1, s2, r2, s3, r3, s4, r4,
+    t_sem, w_sem, s0, r0, s1, r1, s5, r5, s2, r2, s3, r3, s4, r4,
 ):
     row = lax.axis_index("row")
     col = lax.axis_index("col")
@@ -99,7 +99,13 @@
     def copy1(d):
         q = (chip + d) % 8
         return pltpu.make_async_remote_copy(
-            src_ref=acc.at[q], dst_ref=peers.at[d - 1], send_sem=s1.at[d - 1], recv_sem=r1.at[d - 1],
+            src_ref=coded.at[q], dst_ref=codes.at[d - 1], send_sem=s1.at[d - 1], recv_sem=r1.at[d - 1],
+            device_id={"row": 2 * q + core}, device_id_type=MESH)
+
+    def copy5(d):
+        q = (chip + d) % 8
+        return pltpu.make_async_remote_copy(
+            src_ref=unit.at[q], dst_ref=units.at[d - 1], send_sem=s5.at[d - 1], recv_sem=r5.at[d - 1],
             device_id={"row": 2 * q + core}, device_id_type=MESH)
 
     def copy2(d):
@@ -134,11 +140,21 @@
     for d in (4, 3, 5, 2, 6, 1, 7, 0):
         q = (chip + d) % 8
         copy0(q).wait_recv()
-        acc[q] = acc[q] + got[q]
-        if d:
-            copy1(d).start()
+        if d == 0:
+            acc[q] = acc[q] + got[q]
+            continue
+        for p in range(2):
+            for u in range(2):
+                at = pl.ds(64 * u, 64)
+                both = acc[q, p, at, :] + got[q, p, at, :]
+                top = jnp.maximum(jnp.max(jnp.abs(both), axis=0, keepdims=True), 1e-30)
+                coded[q, p, at, :] = jnp.round(both * (32767.0 / top)).astype(jnp.int32).astype(jnp.int16)
+                unit[q, pl.ds(2 * p + u, 1), :] = top * (1.0 / 32767.0)
+        copy1(d).start()
+        copy5(d).start()
     for d in (1, 7, 2, 6, 3, 5, 4):
         copy1(d).wait_recv()
+        copy5(d).wait_recv()
 
     none = jnp.zeros((64, 64), F32)
     wi = jnp.concatenate([none, wi_ref[...]], axis=1)
@@ -149,7 +165,9 @@
     for p in range(2):
         total = acc[chip, p]
         for d in range(7):
-            total = total + peers[d, p]
+            part_of = codes[d, p].astype(jnp.int32).astype(F32)
+            total = total + jnp.concatenate([
+                part_of[:64] * units[d, pl.ds(2 * p, 1), :], part_of[64:] * units[d, pl.ds(2 * p + 1, 1), :]], axis=0)
         gw = hdot(wo, total, NT)
         hw = hdot(total, wi, NT)
         for u in range(2):
@@ -219,6 +237,7 @@
     lax.fori_loop(0, 8, sent0, 0)
     for d in range(1, 8):
         copy1(d).wait_send()
+        copy5(d).wait_send()
         copy2(d).wait_send()
     for d in range(1, 16):
         copy3(d).wait_send()
@@ -262,7 +281,10 @@
             pltpu.VMEM((n_train, depth), BF16),
             pltpu.VMEM((8, 2, 128, 128), F32),
             pltpu.VMEM((8, 2, 128, 128), F32),
-            pltpu.VMEM((7, 2, 128, 128), F32),
+            pltpu.VMEM((8, 2, 128, 128), jnp.int16),
+            pltpu.VMEM((8, 4, 128), F32),
+            pltpu.VMEM((7, 2, 128, 128), jnp.int16),
+            pltpu.VMEM((7, 4, 128), F32),
             pltpu.VMEM((128, 128), F32),
             pltpu.VMEM((8, 16, 128), BF16),
             pltpu.VMEM((7, 16, 128), BF16),
@@ -276,6 +298,7 @@
             dma((8,)), dma((8,)),
             dma((7,)), dma((7,)),
             dma((7,)), dma((7,)),
+            dma((7,)), dma((7,)),
             dma((15,)), dma((15,)),
             dma((7, CHUNKS)), dma((7, CHUNKS)),
         ],

time: 65.2 us -> 60 us (0.920)
  Pallas kernels: 63.3 us -> 58.1 us
    pallas_call x1, Pallas kernels: 54.8 us -> 49.5 us  [on_device(): pl.pallas_call(kernel, out_shape=jax.ShapeDtypeStruct((8, n_train), F32),...]
where the time goes in v3:
time: 60 us; the launch traced here: 59.8 us
  Pallas kernels  58.1 us (97%)
  local copies, waits for them, and re-layouts  1.67 us (3%)
    pallas_call x1, Pallas kernels, on_device(): pl.pallas_call(kernel, out_shape=jax.ShapeDtypeStruct((8, n_train), F32),...  49.5 us
    pallas_call x1, Pallas kernels, on_device(): pl.pallas_call(windows, out_shape=jax.ShapeDtypeStruct((32, 128, 128), F3...  8.55 us
    unnamed x1, local copies, waits for them, and re-layouts  1.67 us

profile of v3, /device:TPU:1, one launch (start us, length us, event | category | flops | bytes accessed | tf_op | source)
XLA Modules:
  0.0 59.8 jit_solution(3615082015908833180)
XLA Ops:
  0.0 8.6 %windows.1.w_ref = f32[32,128,128]{2,1,0:T(8,128)} custom-call(s32[1,64]{1,0:T(1,128)} %lens.1, s32[64]{0:T(128)} %flags.1, bf16[64,1848]{1,0:T(8,128)(2,1)} %bitcast.4, bf16[64,512]{1,0:T(8,128)(2,1)} %bitcast.5, bf16[1848,2048]{1,0:T(8,128)(2,1)} %bitcast.3, bf16[2048,512]{1,0:T(8,128)(2,1)} %grads_hbm.1), custom_call_target="tpu_custom_call" | custom-call | tf_op jit(solution)/shard_map/windows/pallas_call | solution.py:261
  8.6 49.5 %attribute.1 = f32[8,8192]{1,0:T(8,128)} custom-call(f32[32,128,128]{2,1,0:T(8,128)} %windows.1.w_ref, f32[64,64]{1,0:T(8,128)} %wi_ref.1, f32[64,64]{1,0:T(8,128)} %wo_ref.1, bf16[8192,512]{1,0:T(8,128)(2,1)} %train_hbm.1), custom_call_target="tpu_custom_call" | custom-call | tf_op jit(solution)/shard_map/attribute/pallas_call | solution.py:275
  58.1 1.7 %copy.11 = f32[8,8192]{1,0:T(8,128)} copy(f32[8,8192]{1,0:T(8,128)} %attribute.1) | data formatting | bytes 524288

commit v4 on v3

--- a/solution.py
+++ b/solution.py
@@ -10,7 +10,7 @@
 BF16 = jnp.bfloat16
 NT = (((1,), (1,)), ((), ()))
 NN = (((1,), (0,)), ((), ()))
-CHUNKS = 8
+CHUNKS = 4
 
 
 def hdot(a, b, dims):
@@ -60,7 +60,7 @@
             out_ref[j, pl.ds(64 * u, 64), :] = window(2 * j + u)
         return 0
 
-    lax.fori_loop(0, 32, pair, 0, unroll=4)
+    lax.fori_loop(0, 32, pair, 0, unroll=16)
 
 
 def kernel(
@@ -127,14 +127,14 @@
             send_sem=s4.at[d - 1, j], recv_sem=r4.at[d - 1, j],
             device_id={"col": c}, device_id_type=MESH)
 
-    pl.semaphore_wait(barrier, 22)
-
-    for d in (4, 3, 5, 2, 6, 1, 7, 0):
-        copy0((chip + d) % 8).start()
     for q in range(8):
         keep(q).start()
     for k in range(CHUNKS):
         fetch(k).start()
+    pl.semaphore_wait(barrier, 22)
+
+    for d in (4, 3, 5, 2, 6, 1, 7, 0):
+        copy0((chip + d) % 8).start()
     for q in range(8):
         keep(q).wait()
     for d in (4, 3, 5, 2, 6, 1, 7, 0):
@@ -207,7 +207,7 @@
         for c in range(8):
             both = jnp.concatenate([a[8 * c:8 * c + 8], b[8 * c:8 * c + 8]], axis=0)
             send[c, :, pl.ds(lo, width)] = both.astype(BF16)
-        for d in (4, 3, 5, 2, 6, 1, 7):
+        for d in (3, 5, 1, 7, 4, 2, 6):
             copy4(d, j).start()
         part[...] = a
         out_ref[:, pl.ds(lo, width)] = part[own, :]

time: 60 us -> 55.5 us (0.925)
  Pallas kernels: 58.1 us -> 53.3 us
    pallas_call x1, Pallas kernels: 49.5 us -> 46.1 us  [on_device(): pl.pallas_call(kernel, out_shape=jax.ShapeDtypeStruct((8, n_train), F32),...]
    pallas_call x1, Pallas kernels: 8.55 us -> 7.16 us  [on_device(): pl.pallas_call(windows, out_shape=jax.ShapeDtypeStruct((32, 128, 128), F3...]
where the time goes in v4:
time: 55.5 us; the launch traced here: 55 us
  Pallas kernels  53.3 us (96%)
  local copies, waits for them, and re-layouts  1.67 us (3%)
    pallas_call x1, Pallas kernels, on_device(): pl.pallas_call(kernel, out_shape=jax.ShapeDtypeStruct((8, n_train), F32),...  46.1 us
    pallas_call x1, Pallas kernels, on_device(): pl.pallas_call(windows, out_shape=jax.ShapeDtypeStruct((32, 128, 128), F3...  7.16 us
    unnamed x1, local copies, waits for them, and re-layouts  1.67 us

profile of v4, /device:TPU:1, one launch (start us, length us, event | category | flops | bytes accessed | tf_op | source)
XLA Modules:
  0.0 55.0 jit_solution(17420971630056391428)
XLA Ops:
  0.0 7.2 %windows.1.w_ref = f32[32,128,128]{2,1,0:T(8,128)} custom-call(s32[1,64]{1,0:T(1,128)} %lens.1, s32[64]{0:T(128)} %flags.1, bf16[64,1848]{1,0:T(8,128)(2,1)} %bitcast.4, bf16[64,512]{1,0:T(8,128)(2,1)} %bitcast.5, bf16[1848,2048]{1,0:T(8,128)(2,1)} %bitcast.3, bf16[2048,512]{1,0:T(8,128)(2,1)} %grads_hbm.1), custom_call_target="tpu_custom_call" | custom-call | tf_op jit(solution)/shard_map/windows/pallas_call | solution.py:261
  7.2 46.1 %attribute.1 = f32[8,8192]{1,0:T(8,128)} custom-call(f32[32,128,128]{2,1,0:T(8,128)} %windows.1.w_ref, f32[64,64]{1,0:T(8,128)} %wi_ref.1, f32[64,64]{1,0:T(8,128)} %wo_ref.1, bf16[8192,512]{1,0:T(8,128)(2,1)} %train_hbm.1), custom_call_target="tpu_custom_call" | custom-call | tf_op jit(solution)/shard_map/attribute/pallas_call | solution.py:275
  53.3 1.7 %copy.11 = f32[8,8192]{1,0:T(8,128)} copy(f32[8,8192]{1,0:T(8,128)} %attribute.1) | data formatting | bytes 524288
